TPU v7x, 256 devices: a whole 4x4x8 slice. The times are simulated.
256 devices in a mesh: dp: 4 (over x), tensor: 64 (over y, z, core).
Axes of the slice: x: 4, y: 4, z: 8, core: 2. Of those that a mesh axis runs over, the one named last changes fastest.
Arguments:
- grad_out: bfloat16 [4096, 8192], P('dp', 'tensor'), may hold values from -6 to 6
- acts: bfloat16 [4096, 16384], P('dp', 'tensor'), may hold values from -6 to 6
- weight: bfloat16 [8192, 16384], P('tensor'), may hold values from -0.078125 to 0.078125
- block_mask: int32 [64, 128], replicated, may hold values from 0 to 1, as said below
Outputs:
- grad_acts: bfloat16 [4096, 16384], P('dp', 'tensor')
- grad_weight: float32 [8192, 16384], P(('dp', 'tensor'))
Inputs may be any that keep to these rules, and one draw needn't show every extreme that they name: `block_mask`: kept shares differ between groups of 2 consecutive block columns, from about three twentieths to nine twentieths.
All inputs are finite; a program needn't handle non-finite values.
Results may differ from a plain program's by a relative error of at most 0.001.
Values may be sent and summed in bfloat16 or wider, within the bound.
A program may use at most 128 MiB of HBM per device.

v0:
```python
import jax
import jax.numpy as jnp
from jax import lax
from jax.sharding import PartitionSpec as P


def expand_mask(mask, side):
    rows, cols = mask.shape
    full = jnp.broadcast_to(mask[:, None, :, None], (rows, side, cols, side))
    return full.reshape(rows * side, cols * side)


def body(grad_out, acts, weight, block_mask):
    tensor_count = lax.axis_size("tensor")
    group_count = lax.axis_size("dp")
    position = lax.axis_index("tensor")
    d_tile = weight.shape[0]
    full_width = weight.shape[1]
    ff_tile = acts.shape[1]
    side = full_width // block_mask.shape[1]
    total_rows = d_tile * tensor_count
    row_mask = lax.dynamic_slice_in_dim(block_mask, position * (d_tile // side), d_tile // side, 0)
    kept = weight * expand_mask(row_mask, side).astype(jnp.bfloat16)
    columns = lax.all_to_all(kept, "tensor", split_axis=1, concat_axis=0, tiled=True)
    piece = lax.all_gather(grad_out, "tensor", axis=1, tiled=True)
    input_grad = jnp.dot(piece, columns, preferred_element_type=jnp.float32)
    grad_rows = lax.dot_general(
        piece, acts, (((0,), (0,)), ((), ())), preferred_element_type=jnp.float32
    )
    weight_grad = grad_rows
    input_grad, weight_grad = (input_grad, weight_grad)
    grad_acts = input_grad.astype(jnp.bfloat16)
    col_mask = lax.dynamic_slice_in_dim(
        block_mask, position * (ff_tile // side), ff_tile // side, 1
    )
    scale_factor = 1.0 / (grad_out.shape[0] * group_count) ** 0.5
    weight_grad = weight_grad * expand_mask(col_mask, side).astype(jnp.float32) * scale_factor
    quarter = total_rows // (group_count * tensor_count)
    reordered = weight_grad.reshape(group_count, tensor_count, quarter, ff_tile)
    reordered = jnp.transpose(reordered, (1, 0, 2, 3)).reshape(total_rows, ff_tile)
    owned = lax.all_to_all(reordered, "tensor", split_axis=0, concat_axis=1, tiled=True)
    grad_weight = lax.psum_scatter(owned, "dp", scatter_dimension=0, tiled=True)
    return (grad_acts, grad_weight)


def solution(mesh):
    in_specs = (P("dp", "tensor"), P("dp", "tensor"), P("tensor", None), P())
    out_specs = (P("dp", "tensor"), P(("dp", "tensor"), None))
    return jax.shard_map(body, mesh=mesh, in_specs=in_specs, out_specs=out_specs, check_vma=False)
```

profile of v0, /device:TPU:1, one launch (start us, length us, event | category | flops | bytes accessed | tf_op | source)
XLA Modules:
  0.0 497.6 jit_solution(10132291511642374837)
XLA Ops:
  7.2 0.0 copy-start
  7.2 0.0 all-gather.2.cloned.1.call-start
  7.2 0.7 all-gather.2.cloned.1.call-update
  7.9 0.0 reduce-scatter.4.cloned.1.call-start
  8.0 0.8 dynamic-slice_convert_fusion
  8.8 113.1 %all-gather.2.cloned.1.call-done = bf16[1024,8192]{1,0:T(8,128)(2,1)} async-done(((bf16[1024,128]{1,0:T(8,128)(2,1)}), bf16[1024,8192]{1,0:T(8,128)(2,1)}) %all-gather.2.cloned.1.call-update) | async-done | bytes 16777232 | tf_op jit(solution)/shard_map/all_gather | solution.py:25
  121.9 5.5 %broadcast_in_dim.16 = f32[64,128,2,128]{3,2,1,0:T(2,128)} broadcast(f32[64,2]{1,0:T(8,128)S(1)} %dynamic-slice_convert_fusion), dimensions={0,2} | broadcast | bytes 8389120 | tf_op jit(solution)/shard_map/broadcast_in_dim | solution.py:9
  127.4 0.0 copy-done
  127.4 13.7 %fusion = f32[8192,256]{1,0:T(8,128)S(1)} fusion(bf16[1024,8192]{1,0:T(8,128)(2,1)} %all-gather.2.cloned.1.call-done, bf16[1024,256]{1,0:T(8,128)(2,1)S(1)} %copy-done, f32[1024,8,2,128]{3,2,1,0:T(2,128)} %bitcast.29), kind=kOutput, calls=%fused_computation.1 | convolution fusion | flops 4299161600 | bytes 34078720 | tf_op jit(solution)/shard_map/dot_general | solution.py:27
  141.1 1.7 copy.17
  142.7 192.2 %all_to_all.38 = f32[64,128,256]{2,1,0:T(8,128)} all-to-all(f32[64,128,256]{2,1,0:T(8,128)S(1)} %bitcast.24), channel_id=1, replica_groups=mesh['dp'=4,'tensor'=64] {'tensor'}, dimensions={0} | all-to-all | bytes 16777216 | tf_op jit(solution)/shard_map/all_to_all | solution.py:41
  334.9 9.0 %copy.18 = f32[128,64,256]{0,2,1:T(8,128)} copy(f32[128,64,256]{2,0,1:T(8,128)} %bitcast.25) | data formatting | bytes 16777216 | tf_op jit(solution)/shard_map/all_to_all | solution.py:41
  343.9 9.0 %copy.21 = f32[128,16384]{1,0:T(8,128)} copy(f32[128,16384]{0,1:T(8,128)} %bitcast.26) | data formatting | bytes 16777216
  352.8 0.0 reduce-scatter.4.cloned.1.call-update
  352.9 6.4 %copy.15 = bf16[128,16384]{0,1:T(8,128)(2,1)} copy(bf16[128,16384]{1,0:T(8,128)(2,1)} %param.6) | data formatting | bytes 8388608 | tf_op args[2]
  359.2 0.7 convert_bitcast_fusion
  359.9 0.1 broadcast_bitcast_fusion
  360.0 10.0 %broadcast_multiply_fusion = bf16[128,16384]{0,1:T(8,128)(2,1)S(1)} fusion(bf16[128,16384]{0,1:T(8,128)(2,1)} %copy.15, bf16[16384]{0:T(1024)(128)(2,1)S(1)} %broadcast_bitcast_fusion), kind=kLoop, calls=%fused_computation.2 | loop fusion | flops 2097152 | bytes 8421376 | tf_op jit(solution)/shard_map/mul | solution.py:23
  370.0 101.7 %all_to_all.39 = bf16[128,64,256]{0,2,1:T(8,128)(2,1)} all-to-all(bf16[128,64,256]{0,2,1:T(8,128)(2,1)S(1)} %bitcast.27), channel_id=1, replica_groups=mesh['dp'=4,'tensor'=64] {'tensor'}, dimensions={1} | all-to-all | bytes 8388608 | tf_op jit(solution)/shard_map/all_to_all | solution.py:24
  471.7 6.4 %copy.16 = bf16[64,128,256]{2,1,0:T(8,128)(2,1)} copy(bf16[64,128,256]{1,2,0:T(8,128)(2,1)} %bitcast.28) | data formatting | bytes 8388608 | tf_op jit(solution)/shard_map/all_to_all | solution.py:24
  478.1 0.0 copy-start.1
  478.1 11.6 %fusion.1 = bf16[1024,256]{0,1:T(8,128)(2,1)S(1)} fusion(bf16[8192,256]{1,0:T(8,128)(2,1)} %bitcast.31, bf16[1024,8192]{1,0:T(8,128)(2,1)} %all-gather.2.cloned.1.call-done), kind=kOutput, calls=%fused_computation.4 | convolution fusion | flops 4295229440 | bytes 21495808 | tf_op jit(solution)/shard_map/dot_general | solution.py:26
  489.8 1.0 copy.19
  490.8 0.0 reduce-scatter.4.cloned.1.call-done
  490.8 0.0 copy-done.1
Async XLA Ops:
  7.2 120.2 %copy-start = (bf16[1024,256]{1,0:T(8,128)(2,1)S(1)}, bf16[1024,256]{1,0:T(8,128)(2,1)}, u32[]{:S(2)}) copy-start(bf16[1024,256]{1,0:T(8,128)(2,1)} %param.5) | copy-start | bytes 1572868
  7.2 114.8 %all-gather.2.cloned.1.call-start = ((), (), s32[]{:S(2)}) async-start(), calls=%async_computation.3 | async-start | bytes 17039360 | tf_op jit(solution)/shard_map/all_gather | solution.py:25
  7.9 482.8 %reduce-scatter.4.cloned.1.call-start = ((), (), s32[]{:S(2)}) async-start(), calls=%async_computation.4 | async-start | bytes 10485760
  478.1 12.7 %copy-start.1 = (bf16[1024,256]{1,0:T(8,128)(2,1)S(1)}, bf16[1024,256]{1,0:T(8,128)(2,1)}, u32[]{:S(2)}) copy-start(bf16[1024,256]{1,0:T(8,128)(2,1)} %param.5) | copy-start | bytes 1572868
Sparse Core Ops, SparseCore 0:
  10.6 111.3 all-gather.1
  353.0 79.4 reduce-scatter.3
where the time goes:
time: 498 us
  blocking collectives  294 us (59%)
  waiting for transfers between devices  114 us (23%)
  local copies, waits for them, and re-layouts  38.9 us (8%)
  matrix products  25.3 us (5%)
  between operations  14.1 us (3%)
  other arithmetic  11.6 us (2%)
    all_to_all x1, blocking collectives, body(): lax.all_to_all(reordered, 'tensor', split_axis=0, concat_axis=1, tiled=True)  192 us
    all_gather x1, waiting for transfers between devices, body(): piece = lax.all_gather(grad_out, 'tensor', axis=1, tiled=True)  113 us
    all_to_all x1, blocking collectives, body(): lax.all_to_all(kept, 'tensor', split_axis=1, concat_axis=0, tiled=True)  102 us
    unnamed x7, local copies, waits for them, and re-layouts  16.3 us
    dot_general x1, matrix products, body(): lax.dot_general(piece, acts, (((0,), (0,)), ((), ())), preferred_element_...  13.7 us
    dot_general x1, matrix products, body(): input_grad = jnp.dot(piece, columns, preferred_element_type=jnp.float32)  11.6 us
    mul x1, other arithmetic, body(): kept = weight * expand_mask(row_mask, side).astype(jnp.bfloat16)  10 us
  transfers between devices with their start and end apart: 2, of which 1 were waited for; matrix products, arithmetic and copies ran while one was open for 7% of the time, Pallas kernels for 0%

commit v1 on v0

--- a/solution.py
+++ b/solution.py
@@ -2,6 +2,16 @@
 import jax.numpy as jnp
 from jax import lax
 from jax.sharding import PartitionSpec as P
+
+advance_records = lambda field_in, which_axis: jnp.concatenate(
+    jax.lax.all_to_all(
+        jnp.stack([field_in] * jax.lax.axis_size(which_axis), axis=0),
+        which_axis,
+        split_axis=0,
+        concat_axis=0,
+    ),
+    1,
+)
 
 
 def expand_mask(mask, side):
@@ -22,7 +32,7 @@
     row_mask = lax.dynamic_slice_in_dim(block_mask, position * (d_tile // side), d_tile // side, 0)
     kept = weight * expand_mask(row_mask, side).astype(jnp.bfloat16)
     columns = lax.all_to_all(kept, "tensor", split_axis=1, concat_axis=0, tiled=True)
-    piece = lax.all_gather(grad_out, "tensor", axis=1, tiled=True)
+    piece = advance_records(grad_out, "tensor")
     input_grad = jnp.dot(piece, columns, preferred_element_type=jnp.float32)
     grad_rows = lax.dot_general(
         piece, acts, (((0,), (0,)), ((), ())), preferred_element_type=jnp.float32

time: 498 us -> 780 us (1.57)
  waiting for transfers between devices: 114 us -> 365 us
  local copies, waits for them, and re-layouts: 38.9 us -> 61.8 us
  starting transfers between devices: 0.08 us -> 13.5 us
    all_to_all x0 -> x1, waiting for transfers between devices: none -> 365 us  [jax.lax.all_to_all(jnp.stack([field_in] * jax.lax.axis_size(which_axis),...]
    all_gather x1 -> x0, waiting for transfers between devices: 113 us -> none  [body(): piece = lax.all_gather(grad_out, 'tensor', axis=1, tiled=True)]
    reshape x0 -> x1, local copies, waits for them, and re-layouts: none -> 22.4 us  [jnp.concatenate(jax.lax.all_to_all(jnp.stack([field_in] * jax.lax.axis_si...]
    all_to_all x0 -> x1, starting transfers between devices: none -> 13.5 us  [jax.lax.all_to_all(jnp.stack([field_in] * jax.lax.axis_size(which_axis),...]
    unnamed x7 -> x8, local copies, waits for them, and re-layouts: 16.3 us -> 9.98 us
  transfers between devices with their start and end apart: 2 -> 2, of which waited for: 1 -> 1; matrix products, arithmetic and copies ran while one was open for 7% -> 3% of each run, Pallas kernels for 0% -> 0%
where the time goes in v1:
time: 780 us; the launch traced here: 779 us
  waiting for transfers between devices  365 us (47%)
  blocking collectives  294 us (38%)
  local copies, waits for them, and re-layouts  61.8 us (8%)
  matrix products  24.7 us (3%)
  between operations  14.1 us (2%)
  starting transfers between devices  13.5 us (2%)
    all_to_all x1, waiting for transfers between devices, jax.lax.all_to_all(jnp.stack([field_in] * jax.lax.axis_size(which_axis),...  365 us
    all_to_all x1, blocking collectives, body(): lax.all_to_all(reordered, 'tensor', split_axis=0, concat_axis=1, tiled=True)  192 us
    all_to_all x1, blocking collectives, body(): lax.all_to_all(kept, 'tensor', split_axis=1, concat_axis=0, tiled=True)  102 us
    reshape x1, local copies, waits for them, and re-layouts, jnp.concatenate(jax.lax.all_to_all(jnp.stack([field_in] * jax.lax.axis_si...  22.4 us
  transfers between devices with their start and end apart: 2, of which 1 were waited for; matrix products, arithmetic and copies ran while one was open for 3% of the time, Pallas kernels for 0%

profile of v1, /device:TPU:1, one launch (start us, length us, event | category | flops | bytes accessed | tf_op | source)
XLA Modules:
  0.0 778.7 jit_solution(13017810349199021666)
XLA Ops:
  7.2 0.0 copy-start
  7.2 7.0 stack.2
  14.2 0.0 copy-start.2
  14.2 13.5 %all-to-all-start.1 = ((bf16[64,1024,128]{2,1,0:T(8,128)(2,1)}), bf16[64,1024,128]{2,1,0:T(8,128)(2,1)}, u32[]{:S(2)}, u32[]{:S(2)}) async-start(bf16[64,1024,128]{2,1,0:T(8,128)(2,1)} %stack.2), calls=%async_computation.1 | async-start | bytes 33554432 | tf_op jit(solution)/shard_map/all_to_all | solution.py:7
  27.7 0.0 reduce-scatter.4.cloned.1.call-start
  27.7 0.0 copy-done.2
  27.7 0.1 dynamic-slice_convert_fusion
  27.8 365.4 %all-to-all-done.1 = bf16[64,1024,128]{2,1,0:T(8,128)(2,1)} async-done(((bf16[64,1024,128]{2,1,0:T(8,128)(2,1)}), bf16[64,1024,128]{2,1,0:T(8,128)(2,1)}, u32[]{:S(2)}, u32[]{:S(2)}) %all-to-all-start.1) | async-done | bytes 16777248 | tf_op jit(solution)/shard_map/all_to_all | solution.py:7
  393.2 22.4 %copy.19 = bf16[1024,64,128]{0,2,1:T(8,128)(2,1)} copy(bf16[1024,64,128]{2,0,1:T(8,128)(2,1)} %bitcast.4) | data formatting | bytes 33554432 | tf_op jit(solution)/shard_map/reshape | solution.py:6
  415.6 5.4 broadcast_in_dim.16
  421.0 0.0 copy-done
  421.0 13.1 %fusion = f32[8192,256]{1,0:T(8,128)S(1)} fusion(bf16[1024,8192]{0,1:T(8,128)(2,1)} %bitcast.39, bf16[1024,256]{1,0:T(8,128)(2,1)S(1)} %copy-done, f32[1024,8,2,128]{3,2,1,0:T(2,128)} %bitcast.40), kind=kOutput, calls=%fused_computation.1 | convolution fusion | flops 4299161600 | bytes 34078720 | tf_op jit(solution)/shard_map/dot_general | solution.py:37
  434.1 1.7 copy.20
  435.8 192.1 %all_to_all.40 = f32[64,128,256]{2,1,0:T(8,128)} all-to-all(f32[64,128,256]{2,1,0:T(8,128)S(1)} %bitcast.42), channel_id=1, replica_groups=mesh['dp'=4,'tensor'=64] {'tensor'}, dimensions={0} | all-to-all | bytes 16777216 | tf_op jit(solution)/shard_map/all_to_all | solution.py:51
  627.8 9.0 %copy.21 = f32[128,64,256]{0,2,1:T(8,128)} copy(f32[128,64,256]{2,0,1:T(8,128)} %bitcast.43) | data formatting | bytes 16777216 | tf_op jit(solution)/shard_map/all_to_all | solution.py:51
  636.8 9.0 %copy.24 = f32[128,16384]{1,0:T(8,128)} copy(f32[128,16384]{0,1:T(8,128)} %bitcast.44) | data formatting | bytes 16777216
  645.8 0.0 reduce-scatter.4.cloned.1.call-update
  645.8 0.1 broadcast_bitcast_fusion
  645.9 4.7 broadcast_multiply_fusion
  650.6 6.4 copy.18
  657.0 0.0 copy-start.1
  657.0 102.4 %all_to_all.41 = bf16[128,64,256]{0,2,1:T(8,128)(2,1)} all-to-all(bf16[128,64,256]{0,2,1:T(8,128)(2,1)} %bitcast.45), channel_id=1, replica_groups=mesh['dp'=4,'tensor'=64] {'tensor'}, dimensions={1} | all-to-all | bytes 8388608 | tf_op jit(solution)/shard_map/all_to_all | solution.py:34
  759.3 11.6 %fusion.9 = bf16[1024,256]{0,1:T(8,128)(2,1)S(1)} fusion(bf16[128,64,256]{0,2,1:T(8,128)(2,1)} %all_to_all.41, bf16[64,1024,128]{2,1,0:T(8,128)(2,1)} %all-to-all-done.1), kind=kOutput, calls=%fused_computation.7 | convolution fusion | flops 4295229440 | bytes 21495808 | tf_op jit(solution)/shard_map/dot_general | solution.py:36
  770.9 1.0 copy.22
  771.9 0.0 reduce-scatter.4.cloned.1.call-done
  771.9 0.0 copy-done.1
  (1 shorter events, 0.0 us)
Async XLA Ops:
  7.2 413.8 %copy-start = (bf16[1024,256]{1,0:T(8,128)(2,1)S(1)}, bf16[1024,256]{1,0:T(8,128)(2,1)}, u32[]{:S(2)}) copy-start(bf16[1024,256]{1,0:T(8,128)(2,1)} %param.5) | copy-start | bytes 1572868
  14.2 13.5 %copy-start.2 = (s32[64,128]{1,0:T(8,128)S(1)}, s32[64,128]{1,0:T(8,128)}, u32[]{:S(2)}) copy-start(s32[64,128]{1,0:T(8,128)} %param.7) | copy-start | bytes 98308
  14.2 379.0 %all-to-all-start.1 = ((bf16[64,1024,128]{2,1,0:T(8,128)(2,1)}), bf16[64,1024,128]{2,1,0:T(8,128)(2,1)}, u32[]{:S(2)}, u32[]{:S(2)}) async-start(bf16[64,1024,128]{2,1,0:T(8,128)(2,1)} %stack.2), calls=%async_computation.1 | async-start | bytes 33554432 | tf_op jit(solution)/shard_map/all_to_all | solution.py:7
  27.7 744.2 %reduce-scatter.4.cloned.1.call-start = ((), (), s32[]{:S(2)}) async-start(), calls=%async_computation.4 | async-start | bytes 10485760
  657.0 114.9 %copy-start.1 = (bf16[1024,256]{1,0:T(8,128)(2,1)S(1)}, bf16[1024,256]{1,0:T(8,128)(2,1)}, u32[]{:S(2)}) copy-start(bf16[1024,256]{1,0:T(8,128)(2,1)} %param.5) | copy-start | bytes 1572868
Sparse Core Ops, SparseCore 0:
  645.9 79.5 reduce-scatter.3
